TPU v7x, 128 devices: a whole 4x4x4 slice. The times are simulated.
128 devices in a mesh: row: 32 (over y, z, core), col: 4 (over x).
Axes of the slice: x: 4, y: 4, z: 4, core: 2. Of those that a mesh axis runs over, the one named last changes fastest.
Arguments:
- matrix: float32 [16384, 16, 512], P('row', 'col'), may hold values from -200 to 200, as said below
Outputs:
- factored: float32 [16384, 16, 512], P('row', 'col')
- upper_rows: float32 [2, 512, 16, 512], P(None, 'row', 'col')
Inputs may be any that keep to these rules, and one draw needn't show every extreme that they name: `matrix`: Real-valued entries; every panel has full column rank.
All inputs are finite; a program needn't handle non-finite values.
Results may differ from a plain program's by a relative error of at most 0.0001.
Values sent between devices are 32-bit elements; how exact they have to be, the bound alone decides.
A program may use at most 128 MiB of HBM per device.

v0:
```python
import jax
import jax.numpy as jnp
from jax import lax
from jax.sharding import PartitionSpec as P

PANELS = 2
HIGH = lax.Precision.HIGHEST


def spread(value, axis, root):
    mine = lax.axis_index(axis) == root
    return lax.psum(jnp.where(mine, value, jnp.zeros_like(value)), axis)


def right_solve(lower, block):
    eye = jnp.eye(lower.shape[0], dtype=jnp.float32)
    inverse = lax.linalg.triangular_solve(lower, eye, left_side=True, lower=True)
    return jnp.dot(block, inverse.T, precision=HIGH)


def gram_of(block):
    return jnp.dot(block.T, block, precision=HIGH)


def on_device(matrix):
    work = matrix
    row_dev, blocks, width = matrix.shape
    half = width // 2
    n_row = lax.axis_size("row")
    n_col = lax.axis_size("col")
    my_col = lax.axis_index("col")
    my_row = lax.axis_index("row")
    share = width // n_row
    scale = jnp.sqrt(jnp.float32(row_dev * n_row))
    number = jnp.arange(blocks) * n_col + my_col
    pieces = []
    for k in range(PANELS):
        root = k % n_col
        slot = k // n_col
        owner = my_col == root
        panel = work[:, slot, :]
        first = panel[:, :half]
        second = panel[:, half:]
        lower_one = jnp.linalg.cholesky(lax.psum(gram_of(first), "row"))
        basis_one = right_solve(lower_one, first)
        inner = lax.psum(jnp.dot(basis_one.T, second, precision=HIGH), "row")
        rest = second - jnp.dot(basis_one, inner, precision=HIGH)
        lower_two = jnp.linalg.cholesky(lax.psum(gram_of(rest), "row"))
        basis_two = right_solve(lower_two, rest)
        local_basis = jnp.concatenate([basis_one, basis_two], axis=1)
        top = jnp.concatenate([lower_one.T, inner], axis=1)
        bottom = jnp.concatenate([jnp.zeros((half, half), jnp.float32), lower_two.T], axis=1)
        upper = jnp.concatenate([top, bottom], axis=0)
        basis = spread(local_basis, "col", root)
        keep = (number > k).astype(jnp.float32)
        terms = jnp.einsum("rk,rbc->kbc", basis, work, precision=HIGH) * keep[None, :, None]
        weights = lax.psum(terms, "row")
        mine = lax.dynamic_slice_in_dim(weights, my_row * share, share, 0)
        work = work - jnp.einsum("rk,kbc->rbc", basis, weights, precision=HIGH)
        work = work.at[:, slot, :].set(jnp.where(owner, basis * scale, work[:, slot, :]))
        upper_share = lax.dynamic_slice_in_dim(upper, my_row * share, share, 0)
        mine = mine.at[:, slot, :].set(jnp.where(owner, upper_share, mine[:, slot, :]))
        pieces.append(mine)
    return (work, jnp.stack(pieces, axis=0))


def solution(mesh):
    placed = (P("row", "col", None),)
    return jax.shard_map(
        on_device,
        mesh=mesh,
        in_specs=placed,
        out_specs=(P("row", "col", None), P(None, "row", "col", None)),
        check_vma=False,
    )
```

profile of v0, /device:TPU:1, one launch (start us, length us, event | category | flops | bytes accessed | tf_op | source)
XLA Modules:
  0.0 1277.8 jit_solution(5746735367781790815)
XLA Ops:
  7.2 2.9 slice.146
  10.2 1.7 fusion.18
  12.0 105.9 %all-reduce.14.cloned.1.call-done = f32[256,256]{0,1:T(8,128)} async-done(((f32[256,256]{0,1:T(8,128)}), f32[256,256]{0,1:T(8,128)}) %all-reduce.14.cloned.1.call-update) | async-done | bytes 262160 | tf_op jit(solution)/shard_map/psum | solution.py:44
  120.0 11.7 cholesky.214
  131.7 9.8 custom-call.17
  142.0 11.7 cholesky.231
  156.0 4.3 while.12
  156.8 1.4 bitcast_dynamic-update-slice_fusion.9
  158.9 1.4 bitcast_dynamic-update-slice_fusion.9
  160.3 19.7 %custom-call.18 = f32[2,128,128]{1,2,0:T(8,128)S(1)} custom-call(f32[2,128,128]{2,1,0:T(8,128)S(1)} %get-tuple-element.78), custom_call_target="InvertDiagBlocksLowerTriangular" | custom-call | tf_op jit(solution)/shard_map/triangular_solve/custom-call.0 | solution.py:17
  181.5 1.7 fusion.14
  183.3 102.1 %all-reduce.16.cloned.1.call-done = f32[256,256]{0,1:T(8,128)} async-done(((f32[256,256]{0,1:T(8,128)}), f32[256,256]{0,1:T(8,128)}) %all-reduce.16.cloned.1.call-update) | async-done | bytes 262160 | tf_op jit(solution)/shard_map/psum | solution.py:46
  285.4 1.9 convolution_subtract_fusion.3
  287.4 1.7 fusion.94
  289.6 101.7 %all-reduce.18.cloned.1.call-done = f32[256,256]{0,1:T(8,128)} async-done(((f32[256,256]{0,1:T(8,128)}), f32[256,256]{0,1:T(8,128)}) %all-reduce.18.cloned.1.call-update) | async-done | bytes 262160 | tf_op jit(solution)/shard_map/psum | solution.py:48
  393.4 11.7 cholesky.248
  405.1 9.8 custom-call.19
  415.6 11.7 cholesky.265
  430.1 4.3 while.13
  434.4 19.7 %custom-call.20 = f32[2,128,128]{1,2,0:T(8,128)S(1)} custom-call(f32[2,128,128]{2,1,0:T(8,128)S(1)} %get-tuple-element.79), custom_call_target="InvertDiagBlocksLowerTriangular" | custom-call | tf_op jit(solution)/shard_map/triangular_solve/custom-call.0 | solution.py:17
  456.8 5.2 copy.42
  462.1 38.5 %all-reduce.20.cloned.1.call-done = f32[512,512]{0,1:T(8,128)} async-done(((f32[512,512]{0,1:T(8,128)}), f32[512,512]{0,1:T(8,128)}) %all-reduce.20.cloned.1.call-update) | async-done | bytes 1048592 | tf_op jit(solution)/shard_map/psum | solution.py:12
  500.6 10.2 convolution_multiply_fusion.1
  510.8 114.6 %all-reduce.22.cloned.1.call-done = f32[512,4,512]{0,2,1:T(8,128)} async-done(((f32[512,4,512]{0,2,1:T(8,128)}), f32[512,4,512]{0,2,1:T(8,128)}) %all-reduce.22.cloned.1.call-update) | async-done | bytes 4194320 | tf_op jit(solution)/shard_map/psum | solution.py:57
  625.4 9.2 convolution_subtract_fusion.1
  634.7 2.0 copy-done
  638.7 101.8 %all-reduce.24.cloned.1.call-done = f32[256,256]{0,1:T(8,128)} async-done(((f32[256,256]{0,1:T(8,128)}), f32[256,256]{0,1:T(8,128)}) %all-reduce.24.cloned.1.call-update) | async-done | bytes 262160 | tf_op jit(solution)/shard_map/psum | solution.py:44
  742.5 11.7 cholesky.282
  754.3 9.8 custom-call.21
  764.6 11.7 cholesky.299
  779.7 3.9 while.14
  783.5 19.7 %custom-call.22 = f32[2,128,128]{1,2,0:T(8,128)S(1)} custom-call(f32[2,128,128]{2,1,0:T(8,128)S(1)} %get-tuple-element.80), custom_call_target="InvertDiagBlocksLowerTriangular" | custom-call | tf_op jit(solution)/shard_map/triangular_solve/custom-call.0 | solution.py:17
  806.1 102.1 %all-reduce.26.cloned.1.call-done = f32[256,256]{0,1:T(8,128)} async-done(((f32[256,256]{0,1:T(8,128)}), f32[256,256]{0,1:T(8,128)}) %all-reduce.26.cloned.1.call-update) | async-done | bytes 262160 | tf_op jit(solution)/shard_map/psum | solution.py:46
  908.2 1.6 convolution_subtract_fusion.2
  911.4 102.1 %all-reduce.28.cloned.1.call-done = f32[256,256]{0,1:T(8,128)} async-done(((f32[256,256]{0,1:T(8,128)}), f32[256,256]{0,1:T(8,128)}) %all-reduce.28.cloned.1.call-update) | async-done | bytes 262160 | tf_op jit(solution)/shard_map/psum | solution.py:48
  1015.5 11.7 cholesky.316
  1027.3 9.8 custom-call.23
  1037.8 11.7 cholesky.333
  1052.9 4.1 while.15
  1057.0 19.7 %custom-call.24 = f32[2,128,128]{1,2,0:T(8,128)S(1)} custom-call(f32[2,128,128]{2,1,0:T(8,128)S(1)} %get-tuple-element.81), custom_call_target="InvertDiagBlocksLowerTriangular" | custom-call | tf_op jit(solution)/shard_map/triangular_solve/custom-call.0 | solution.py:17
  1080.4 42.7 %all-reduce.30.cloned.1.call-done = f32[512,512]{0,1:T(8,128)} async-done(((f32[512,512]{0,1:T(8,128)}), f32[512,512]{0,1:T(8,128)}) %all-reduce.30.cloned.1.call-update) | async-done | bytes 1048592 | tf_op jit(solution)/shard_map/psum | solution.py:12
  1123.1 10.2 convolution_multiply_fusion
  1135.6 1.7 constant_dynamic-slice_fusion.5
  1137.6 110.4 %all-reduce.32.cloned.1.call-done = f32[512,4,512]{0,2,1:T(8,128)} async-done(((f32[512,4,512]{0,2,1:T(8,128)}), f32[512,4,512]{0,2,1:T(8,128)}) %all-reduce.32.cloned.1.call-update) | async-done | bytes 4194320 | tf_op jit(solution)/shard_map/psum | solution.py:57
  1249.4 1.6 constant_dynamic-slice_fusion.4
  1252.2 10.5 convolution_subtract_fusion
  1262.7 2.4 fusion.2
  1265.1 5.4 copy.60
  (145 shorter events, 50.4 us)
Async XLA Ops:
  7.2 110.7 %all-reduce.14.cloned.1.call-start = ((), (), s32[]{:S(2)}) async-start(), calls=%async_computation | async-start | bytes 524288 | tf_op jit(solution)/shard_map/psum | solution.py:44
  11.9 273.5 %all-reduce.16.cloned.1.call-start = ((), (), s32[]{:S(2)}) async-start(), calls=%async_computation.1 | async-start | bytes 524288 | tf_op jit(solution)/shard_map/psum | solution.py:46
  183.3 208.0 %all-reduce.18.cloned.1.call-start = ((), (), s32[]{:S(2)}) async-start(), calls=%async_computation.2 | async-start | bytes 524288 | tf_op jit(solution)/shard_map/psum | solution.py:48
  289.1 211.4 %all-reduce.20.cloned.1.call-start = ((), (), s32[]{:S(2)}) async-start(), calls=%async_computation.3 | async-start | bytes 2097152 | tf_op jit(solution)/shard_map/psum | solution.py:12
  456.8 168.6 %all-reduce.22.cloned.1.call-start = ((), (), s32[]{:S(2)}) async-start(), calls=%async_computation.4 | async-start | bytes 8388608 | tf_op jit(solution)/shard_map/psum | solution.py:57
  510.7 114.7 %copy-start.2 = (f32[512,512]{0,1:T(8,128)S(1)}, f32[512,512]{0,1:T(8,128)}, u32[]{:S(2)}) copy-start(f32[512,512]{0,1:T(8,128)} %all-reduce.20.cloned.1.call-done) | copy-start | bytes 3145732
  510.7 229.7 %all-reduce.24.cloned.1.call-start = ((), (), s32[]{:S(2)}) async-start(), calls=%async_computation.5 | async-start | bytes 524288 | tf_op jit(solution)/shard_map/psum | solution.py:44
  634.6 2.0 copy-start
  638.2 270.0 %all-reduce.26.cloned.1.call-start = ((), (), s32[]{:S(2)}) async-start(), calls=%async_computation.6 | async-start | bytes 524288 | tf_op jit(solution)/shard_map/psum | solution.py:46
  806.1 207.4 %all-reduce.28.cloned.1.call-start = ((), (), s32[]{:S(2)}) async-start(), calls=%async_computation.7 | async-start | bytes 524288 | tf_op jit(solution)/shard_map/psum | solution.py:48
  911.2 212.0 %all-reduce.30.cloned.1.call-start = ((), (), s32[]{:S(2)}) async-start(), calls=%async_computation.8 | async-start | bytes 2097152 | tf_op jit(solution)/shard_map/psum | solution.py:12
  1079.3 168.7 %all-reduce.32.cloned.1.call-start = ((), (), s32[]{:S(2)}) async-start(), calls=%async_computation.9 | async-start | bytes 8388608 | tf_op jit(solution)/shard_map/psum | solution.py:57
  1133.3 0.9 copy-start.3
  1133.3 114.7 %copy-start.4 = (f32[256,256]{0,1:T(8,128)S(1)}, f32[256,256]{0,1:T(8,128)}, u32[]{:S(2)}) copy-start(f32[256,256]{0,1:T(8,128)} %all-reduce.26.cloned.1.call-done) | copy-start | bytes 786436
  1133.3 114.7 %copy-start.5 = (f32[256,256]{0,1:T(8,128)S(1)}, f32[256,256]{0,1:T(8,128)}, u32[]{:S(2)}) copy-start(f32[256,256]{0,1:T(8,128)} %get-tuple-element.132) | copy-start | bytes 786436
  1133.3 114.7 %copy-start.6 = (f32[256,256]{0,1:T(8,128)S(1)}, f32[256,256]{0,1:T(8,128)}, u32[]{:S(2)}) copy-start(f32[256,256]{0,1:T(8,128)} %get-tuple-element.130) | copy-start | bytes 786436
  1135.6 116.6 %copy-start.1 = (f32[512,512]{0,1:T(8,128)S(1)}, f32[512,512]{0,1:T(8,128)}, u32[]{:S(2)}) copy-start(f32[512,512]{0,1:T(8,128)} %all-reduce.30.cloned.1.call-done) | copy-start | bytes 3145732
Sparse Core Ops, SparseCore 0:
  12.0 105.7 all-reduce.13
  183.4 102.0 all-reduce.15
  289.3 101.9 all-reduce.17
  456.9 43.6 all-reduce.19
  510.9 114.5 all-reduce.21
  638.4 102.0 all-reduce.23
  806.2 101.9 all-reduce.25
  911.4 101.9 all-reduce.27
  1079.4 43.6 all-reduce.29
  1133.5 114.5 all-reduce.31
where the time goes:
time: 1290 us; the launch traced here: 1280 us
  waiting for transfers between devices  922 us (71%)
  other arithmetic  229 us (18%)
  matrix products  60.8 us (5%)
  local copies, waits for them, and re-layouts  43 us (3%)
  between operations  20.3 us (2%)
    psum x2, waiting for transfers between devices, on_device(): weights = lax.psum(terms, 'row')  225 us
    psum x2, waiting for transfers between devices, on_device(): lower_one = jnp.linalg.cholesky(lax.psum(gram_of(first), 'row'))  208 us
    psum x2, waiting for transfers between devices, on_device(): inner = lax.psum(jnp.dot(basis_one.T, second, precision=HIGH), 'row')  204 us
    psum x2, waiting for transfers between devices, on_device(): lower_two = jnp.linalg.cholesky(lax.psum(gram_of(rest), 'row'))  204 us
    psum x2, waiting for transfers between devices, spread(): return lax.psum(jnp.where(mine, value, jnp.zeros_like(value)), axis)  81.2 us
    another operation x5, other arithmetic, right_solve(): lax.linalg.triangular_solve(lower, eye, left_side=True, lower=True)  78.7 us
    another operation x14, other arithmetic, on_device(): lower_two = jnp.linalg.cholesky(lax.psum(gram_of(rest), 'row'))  69.3 us
    another operation x13, other arithmetic, on_device(): lower_one = jnp.linalg.cholesky(lax.psum(gram_of(first), 'row'))  68.6 us
  transfers between devices with their start and end apart: 10, of which 10 were waited for; matrix products, arithmetic and copies ran while one was open for 1% of the time, Pallas kernels for 0%

commit v1 on v0

--- a/solution.py
+++ b/solution.py
@@ -43,7 +43,7 @@
         second = panel[:, half:]
         lower_one = jnp.linalg.cholesky(lax.psum(gram_of(first), "row"))
         basis_one = right_solve(lower_one, first)
-        inner = lax.psum(jnp.dot(basis_one.T, second, precision=HIGH), "row")
+        inner = jnp.sum(lax.all_gather(jnp.dot(basis_one.T, second, precision=HIGH), "row"), axis=0)
         rest = second - jnp.dot(basis_one, inner, precision=HIGH)
         lower_two = jnp.linalg.cholesky(lax.psum(gram_of(rest), "row"))
         basis_two = right_solve(lower_two, rest)

time: 1290 us -> 1190 us (0.922)
  waiting for transfers between devices: 922 us -> 822 us
    psum x2 -> x0, waiting for transfers between devices: 204 us -> none  [on_device(): inner = lax.psum(jnp.dot(basis_one.T, second, precision=HIGH), 'row')]
    all_gather x0 -> x2, waiting for transfers between devices: none -> 106 us  [on_device(): lax.all_gather(jnp.dot(basis_one.T, second, precision=HIGH), 'row')]
where the time goes in v1:
time: 1190 us; the launch traced here: 1180 us
  waiting for transfers between devices  822 us (69%)
  other arithmetic  239 us (20%)
  matrix products  58.5 us (5%)
  local copies, waits for them, and re-layouts  42.9 us (4%)
  between operations  20.2 us (2%)
    psum x2, waiting for transfers between devices, on_device(): weights = lax.psum(terms, 'row')  225 us
    psum x2, waiting for transfers between devices, on_device(): lower_one = jnp.linalg.cholesky(lax.psum(gram_of(first), 'row'))  208 us
    psum x2, waiting for transfers between devices, on_device(): lower_two = jnp.linalg.cholesky(lax.psum(gram_of(rest), 'row'))  203 us
    all_gather x2, waiting for transfers between devices, on_device(): lax.all_gather(jnp.dot(basis_one.T, second, precision=HIGH), 'row')  106 us
    psum x2, waiting for transfers between devices, spread(): return lax.psum(jnp.where(mine, value, jnp.zeros_like(value)), axis)  81.2 us
    another operation x5, other arithmetic, right_solve(): lax.linalg.triangular_solve(lower, eye, left_side=True, lower=True)  78.7 us
    another operation x14, other arithmetic, on_device(): lower_two = jnp.linalg.cholesky(lax.psum(gram_of(rest), 'row'))  69.2 us
    another operation x13, other arithmetic, on_device(): lower_one = jnp.linalg.cholesky(lax.psum(gram_of(first), 'row'))  68.6 us
  transfers between devices with their start and end apart: 10, of which 10 were waited for; matrix products, arithmetic and copies ran while one was open for 1% of the time, Pallas kernels for 0%

profile of v1, /device:TPU:1, one launch (start us, length us, event | category | flops | bytes accessed | tf_op | source)
XLA Modules:
  0.0 1185.0 jit_solution(15816258758011770218)
XLA Ops:
  7.2 2.9 slice.146
  10.2 1.7 fusion.18
  12.0 105.9 %all-reduce.12.cloned.1.call-done = f32[256,256]{0,1:T(8,128)} async-done(((f32[256,256]{0,1:T(8,128)}), f32[256,256]{0,1:T(8,128)}) %all-reduce.12.cloned.1.call-update) | async-done | bytes 262160 | tf_op jit(solution)/shard_map/psum | solution.py:44
  120.0 11.7 cholesky.214
  131.7 9.8 custom-call.17
  142.0 11.7 cholesky.231
  156.7 4.3 while.12
  159.6 1.3 bitcast_dynamic-update-slice_fusion.9
  161.0 19.7 %custom-call.18 = f32[2,128,128]{1,2,0:T(8,128)S(1)} custom-call(f32[2,128,128]{2,1,0:T(8,128)S(1)} %get-tuple-element.78), custom_call_target="InvertDiagBlocksLowerTriangular" | custom-call | tf_op jit(solution)/shard_map/triangular_solve/custom-call.0 | solution.py:17
  183.6 52.8 %all-gather.5.cloned.1.call-done = f32[8192,256]{1,0:T(8,128)} async-done(((f32[256,256]{1,0:T(8,128)}), f32[8192,256]{1,0:T(8,128)}) %all-gather.5.cloned.1.call-update) | async-done | bytes 8388624 | tf_op jit(solution)/shard_map/all_gather | solution.py:46
  236.4 3.9 reduce_sum.18
  241.3 1.7 fusion.94
  243.5 101.4 %all-reduce.14.cloned.1.call-done = f32[256,256]{0,1:T(8,128)} async-done(((f32[256,256]{0,1:T(8,128)}), f32[256,256]{0,1:T(8,128)}) %all-reduce.14.cloned.1.call-update) | async-done | bytes 262160 | tf_op jit(solution)/shard_map/psum | solution.py:48
  347.0 11.7 cholesky.248
  358.7 9.8 custom-call.19
  369.2 11.7 cholesky.265
  384.4 4.3 while.13
  385.2 1.4 bitcast_dynamic-update-slice_fusion.10
  387.3 1.4 bitcast_dynamic-update-slice_fusion.10
  388.7 19.7 %custom-call.20 = f32[2,128,128]{1,2,0:T(8,128)S(1)} custom-call(f32[2,128,128]{2,1,0:T(8,128)S(1)} %get-tuple-element.79), custom_call_target="InvertDiagBlocksLowerTriangular" | custom-call | tf_op jit(solution)/shard_map/triangular_solve/custom-call.0 | solution.py:17
  411.1 5.2 copy.68
  416.4 38.5 %all-reduce.16.cloned.1.call-done = f32[512,512]{0,1:T(8,128)} async-done(((f32[512,512]{0,1:T(8,128)}), f32[512,512]{0,1:T(8,128)}) %all-reduce.16.cloned.1.call-update) | async-done | bytes 1048592 | tf_op jit(solution)/shard_map/psum | solution.py:12
  454.9 10.2 convolution_multiply_fusion.1
  465.1 114.5 %all-reduce.18.cloned.1.call-done = f32[512,4,512]{0,2,1:T(8,128)} async-done(((f32[512,4,512]{0,2,1:T(8,128)}), f32[512,4,512]{0,2,1:T(8,128)}) %all-reduce.18.cloned.1.call-update) | async-done | bytes 4194320 | tf_op jit(solution)/shard_map/psum | solution.py:57
  579.7 9.2 convolution_subtract_fusion.1
  588.9 2.0 copy-done
  592.9 101.8 %all-reduce.20.cloned.1.call-done = f32[256,256]{0,1:T(8,128)} async-done(((f32[256,256]{0,1:T(8,128)}), f32[256,256]{0,1:T(8,128)}) %all-reduce.20.cloned.1.call-update) | async-done | bytes 262160 | tf_op jit(solution)/shard_map/psum | solution.py:44
  696.8 11.7 cholesky.282
  708.5 9.8 custom-call.21
  718.8 11.7 cholesky.299
  733.8 3.8 while.14
  737.6 19.7 %custom-call.22 = f32[2,128,128]{1,2,0:T(8,128)S(1)} custom-call(f32[2,128,128]{2,1,0:T(8,128)S(1)} %get-tuple-element.80), custom_call_target="InvertDiagBlocksLowerTriangular" | custom-call | tf_op jit(solution)/shard_map/triangular_solve/custom-call.0 | solution.py:17
  760.2 52.8 %all-gather.7.cloned.1.call-done = f32[8192,256]{1,0:T(8,128)} async-done(((f32[256,256]{1,0:T(8,128)}), f32[8192,256]{1,0:T(8,128)}) %all-gather.7.cloned.1.call-update) | async-done | bytes 8388624 | tf_op jit(solution)/shard_map/all_gather | solution.py:46
  813.1 3.9 reduce_sum.19
  819.3 101.6 %all-reduce.22.cloned.1.call-done = f32[256,256]{0,1:T(8,128)} async-done(((f32[256,256]{0,1:T(8,128)}), f32[256,256]{0,1:T(8,128)}) %all-reduce.22.cloned.1.call-update) | async-done | bytes 262160 | tf_op jit(solution)/shard_map/psum | solution.py:48
  922.9 11.7 cholesky.316
  934.7 9.8 custom-call.23
  945.2 11.7 cholesky.333
  960.2 4.0 while.15
  964.2 19.7 %custom-call.24 = f32[2,128,128]{1,2,0:T(8,128)S(1)} custom-call(f32[2,128,128]{2,1,0:T(8,128)S(1)} %get-tuple-element.81), custom_call_target="InvertDiagBlocksLowerTriangular" | custom-call | tf_op jit(solution)/shard_map/triangular_solve/custom-call.0 | solution.py:17
  987.7 42.7 %all-reduce.24.cloned.1.call-done = f32[512,512]{0,1:T(8,128)} async-done(((f32[512,512]{0,1:T(8,128)}), f32[512,512]{0,1:T(8,128)}) %all-reduce.24.cloned.1.call-update) | async-done | bytes 1048592 | tf_op jit(solution)/shard_map/psum | solution.py:12
  1030.4 10.2 convolution_multiply_fusion
  1042.9 1.6 constant_dynamic-slice_fusion.5
  1045.0 110.3 %all-reduce.26.cloned.1.call-done = f32[512,4,512]{0,2,1:T(8,128)} async-done(((f32[512,4,512]{0,2,1:T(8,128)}), f32[512,4,512]{0,2,1:T(8,128)}) %all-reduce.26.cloned.1.call-update) | async-done | bytes 4194320 | tf_op jit(solution)/shard_map/psum | solution.py:57
  1156.6 1.6 constant_dynamic-slice_fusion.4
  1159.4 10.5 convolution_subtract_fusion
  1169.9 2.4 fusion.2
  1172.3 5.4 copy.87
  (149 shorter events, 53.4 us)
Async XLA Ops:
  7.2 110.7 %all-reduce.12.cloned.1.call-start = ((), (), s32[]{:S(2)}) async-start(), calls=%async_computation | async-start | bytes 524288 | tf_op jit(solution)/shard_map/psum | solution.py:44
  11.9 224.5 %all-gather.5.cloned.1.call-start = ((), (), s32[]{:S(2)}) async-start(), calls=%async_computation.8 | async-start | bytes 8650752 | tf_op jit(solution)/shard_map/all_gather | solution.py:46
  183.5 161.4 %all-reduce.14.cloned.1.call-start = ((), (), s32[]{:S(2)}) async-start(), calls=%async_computation.1 | async-start | bytes 524288 | tf_op jit(solution)/shard_map/psum | solution.py:48
  243.1 211.8 %all-reduce.16.cloned.1.call-start = ((), (), s32[]{:S(2)}) async-start(), calls=%async_computation.2 | async-start | bytes 2097152 | tf_op jit(solution)/shard_map/psum | solution.py:12
  411.1 168.6 %all-reduce.18.cloned.1.call-start = ((), (), s32[]{:S(2)}) async-start(), calls=%async_computation.3 | async-start | bytes 8388608 | tf_op jit(solution)/shard_map/psum | solution.py:57
  465.0 114.6 %copy-start.2 = (f32[512,512]{0,1:T(8,128)S(1)}, f32[512,512]{0,1:T(8,128)}, u32[]{:S(2)}) copy-start(f32[512,512]{0,1:T(8,128)} %all-reduce.16.cloned.1.call-done) | copy-start | bytes 3145732
  465.1 229.6 %all-reduce.20.cloned.1.call-start = ((), (), s32[]{:S(2)}) async-start(), calls=%async_computation.4 | async-start | bytes 524288 | tf_op jit(solution)/shard_map/psum | solution.py:44
  588.9 2.0 copy-start
  592.5 220.6 %all-gather.7.cloned.1.call-start = ((), (), s32[]{:S(2)}) async-start(), calls=%async_computation.9 | async-start | bytes 8650752 | tf_op jit(solution)/shard_map/all_gather | solution.py:46
  760.2 160.7 %all-reduce.22.cloned.1.call-start = ((), (), s32[]{:S(2)}) async-start(), calls=%async_computation.5 | async-start | bytes 524288 | tf_op jit(solution)/shard_map/psum | solution.py:48
  819.0 211.3 %all-reduce.24.cloned.1.call-start = ((), (), s32[]{:S(2)}) async-start(), calls=%async_computation.6 | async-start | bytes 2097152 | tf_op jit(solution)/shard_map/psum | solution.py:12
  986.5 168.7 %all-reduce.26.cloned.1.call-start = ((), (), s32[]{:S(2)}) async-start(), calls=%async_computation.7 | async-start | bytes 8388608 | tf_op jit(solution)/shard_map/psum | solution.py:57
  1040.5 0.9 copy-start.3
  1040.5 1.0 copy-start.4
  1040.5 114.7 %copy-start.5 = (f32[256,256]{0,1:T(8,128)S(1)}, f32[256,256]{0,1:T(8,128)}, u32[]{:S(2)}) copy-start(f32[256,256]{0,1:T(8,128)} %get-tuple-element.134) | copy-start | bytes 786436
  1040.5 114.7 %copy-start.6 = (f32[256,256]{0,1:T(8,128)S(1)}, f32[256,256]{0,1:T(8,128)}, u32[]{:S(2)}) copy-start(f32[256,256]{0,1:T(8,128)} %get-tuple-element.132) | copy-start | bytes 786436
  1044.5 114.9 %copy-start.1 = (f32[512,512]{0,1:T(8,128)S(1)}, f32[512,512]{0,1:T(8,128)}, u32[]{:S(2)}) copy-start(f32[512,512]{0,1:T(8,128)} %all-reduce.24.cloned.1.call-done) | copy-start | bytes 3145732
Sparse Core Ops, SparseCore 0:
  12.0 105.7 all-reduce.11
  183.6 52.7 all-gather.4
  243.2 101.6 all-reduce.13
  411.2 43.6 all-reduce.15
  465.2 114.4 all-reduce.17
  592.6 102.0 all-reduce.19
  760.3 52.7 all-gather.6
  819.2 101.6 all-reduce.21
  986.7 43.6 all-reduce.23
  1040.7 114.5 all-reduce.25
